TPU v7x, 128 devices: a whole 4x4x4 slice. The times are simulated.
128 devices in a mesh: contour: 4 (over x), clus: 32 (over y, z, core).
Axes of the slice: x: 4, y: 4, z: 4, core: 2. Of those that a mesh axis runs over, the one named last changes fastest.
Arguments:
- probes: float32 [256, 2, 16, 128], P('clus'), may hold values from -18 to 18
- near_blocks: bfloat16 [1024, 27, 2, 128, 128], P(('contour', 'clus')), parts along dimension 0
- near_list: int32 [256, 27], P('clus'), may hold values from 0 to 255, as said below
- near_count: int32 [256], P('clus'), may hold values from 1 to 27
- cluster_rows: int32 [256], P('clus'), may hold values from 64 to 128
- row_basis: bfloat16 [1024, 2, 32, 128], P(('contour', 'clus')), parts along dimension 0, may hold values from -1 to 1
- col_basis: bfloat16 [1024, 2, 32, 128], P(('contour', 'clus')), parts along dimension 0, may hold values from -0.5 to 0.5
- far_list: int32 [256, 32], P('clus'), may hold values from 0 to 255, as said below
- far_coupling: float32 [1024, 32, 2, 32, 32], P(('contour', 'clus')), parts along dimension 0, may hold values from -0.375 to 0.375
- weight: float32 [8], P('contour'), parts along dimension 0, may hold values from -6 to 6
Outputs:
- solution: float32 [1024, 2, 16, 128], P(('contour', 'clus')), parts along dimension 0
- moment: float32 [8, 16, 16], P('contour'), parts along dimension 0
- arnoldi: float32 [16, 16], P('contour'), parts along dimension 0
There are 4 independent parts, one for each index of `contour`. A program takes and returns all parts, laid end to end along the dimension named above; an argument that names none is the same for every part. Nothing has to cross between parts.
Inputs may be any that keep to these rules, and one draw needn't show every extreme that they name: near_list[i, 0] = i; every entry lies within 8 clusters of i. `far_list`: every entry j of cluster i's list has min(|j - i|, 256 - |j - i|) > 8, so no far slot names a cluster of i's near list.
All inputs are finite; a program needn't handle non-finite values.
Results may differ from a plain program's by a relative error of at most 0.0019.
Values may be sent and summed in bfloat16 or wider, within the bound.
No kernel may reach another device: no remote copies, remote signals or barrier semaphores. Data moves between devices by JAX's collectives and lax.ppermute only.
A program may use at most 128 MiB of HBM per device.

v0:
```python
import jax
import jax.numpy as jnp
from jax import lax
from jax.sharding import PartitionSpec as P


def padded_2(cells, sides, width):
    for axis, dim in sides:
        count = lax.axis_size(axis)
        ends = count - 1
        head = lax.slice_in_dim(cells, 0, width, axis=dim)
        tail = lax.slice_in_dim(cells, cells.shape[dim] - width, cells.shape[dim], axis=dim)
        cells = jnp.concatenate(
            [
                lax.ppermute(tail, axis, [(i, (i + 1) % count) for i in range(ends)]),
                cells,
                lax.ppermute(head, axis, [((i + 1) % count, i) for i in range(ends)]),
            ],
            axis=dim,
        )
    return cells


def block_product(blocks, pulled):

    def prod(mat, vec):
        return jnp.einsum("nkrs,nkps->npr", mat, vec, preferred_element_type=jnp.float32)

    real_part = prod(blocks[:, :, 0], pulled[:, :, 0]) - prod(blocks[:, :, 1], pulled[:, :, 1])
    imag_part = prod(blocks[:, :, 0], pulled[:, :, 1]) + prod(blocks[:, :, 1], pulled[:, :, 0])
    return jnp.stack([real_part, imag_part], axis=1)


def basis_contract(basis, narrow):

    def contract(mat, vec):
        return jnp.einsum("nqr,npr->nqp", mat, vec, preferred_element_type=jnp.float32)

    real_part = contract(basis[:, 0], narrow[:, 0]) - contract(basis[:, 1], narrow[:, 1])
    imag_part = contract(basis[:, 0], narrow[:, 1]) + contract(basis[:, 1], narrow[:, 0])
    count = real_part.shape[0]
    return jnp.stack([real_part.reshape(count, -1), imag_part.reshape(count, -1)], axis=1)


def basis_expand(basis, farcoef):

    def expand(mat, vec):
        return jnp.einsum("nqr,nqp->npr", mat, vec, preferred_element_type=jnp.float32)

    real_part = expand(basis[:, 0], farcoef[:, 0]) - expand(basis[:, 1], farcoef[:, 1])
    imag_part = expand(basis[:, 0], farcoef[:, 1]) + expand(basis[:, 1], farcoef[:, 0])
    return jnp.stack([real_part, imag_part], axis=1)


def far_couple(coupling, taken):
    high = lax.Precision.HIGHEST

    def couple(mat, vec):
        return jnp.einsum("nfqs,nfsp->nqp", mat, vec, precision=high)

    real_part = couple(coupling[:, :, 0], taken[:, :, 0]) - couple(
        coupling[:, :, 1], taken[:, :, 1]
    )
    imag_part = couple(coupling[:, :, 0], taken[:, :, 1]) + couple(
        coupling[:, :, 1], taken[:, :, 0]
    )
    return jnp.stack([real_part, imag_part], axis=1)


def inner(left, right):
    real_part = jnp.sum(left[:, 0] * right[:, 0] + left[:, 1] * right[:, 1], axis=(0, 2))
    imag_part = jnp.sum(left[:, 0] * right[:, 1] - left[:, 1] * right[:, 0], axis=(0, 2))
    return (real_part, imag_part)


def squares(field):
    return jnp.sum(field * field, axis=(0, 1, 3))


def scaled(field, real_part, imag_part):
    sr = real_part[None, :, None]
    si = imag_part[None, :, None]
    return jnp.stack(
        [sr * field[:, 0] - si * field[:, 1], sr * field[:, 1] + si * field[:, 0]], axis=1
    )


def shards(
    probes,
    near_blocks,
    near_list,
    near_count,
    cluster_rows,
    row_basis,
    col_basis,
    far_list,
    far_coupling,
    weight,
):
    owned = probes.shape[0]
    nprobe = probes.shape[2]
    width = probes.shape[3]
    rank = col_basis.shape[2]
    first_id = lax.axis_index("clus") * owned
    total_clusters = owned * lax.axis_size("clus")
    rows_iota = lax.broadcasted_iota(jnp.int32, (owned, width), 1)
    row_mask = (rows_iota < cluster_rows[:, None]).astype(jnp.float32)[:, None, None, :]
    slots_iota = lax.broadcasted_iota(jnp.int32, near_list.shape, 1)
    slot_live = slots_iota < near_count[:, None]
    local_ids = near_list - (first_id - owned)

    def operate(field):
        narrow = field.astype(jnp.bfloat16)
        padded = padded_2(narrow, (("clus", 0),), owned)
        pulled = jnp.take(padded, local_ids, axis=0)
        pulled = jnp.where(slot_live[:, :, None, None, None], pulled, jnp.zeros((), jnp.bfloat16))
        near = block_product(near_blocks, pulled)
        coef = basis_contract(col_basis, narrow)
        whole = lax.all_gather(coef, "clus", axis=0, tiled=True)
        whole = whole.reshape(whole.shape[0], 2, rank, nprobe)
        taken = jnp.take(whole, far_list, axis=0)
        farcoef = far_couple(far_coupling, taken)
        farcoef_b = farcoef.astype(jnp.bfloat16)
        far = basis_expand(row_basis, farcoef_b)
        return (near + far) * row_mask

    base = probes * row_mask
    beta = jnp.sqrt(lax.psum(squares(base), "clus") + 1e-06)
    first = base / beta[None, None, :, None]
    image_one = operate(first)
    local_re, local_im = inner(first, image_one)
    proj_re, proj_im = lax.psum((local_re, local_im), "clus")
    remain = image_one - scaled(first, proj_re, proj_im)
    norm_sq = lax.psum(squares(remain), "clus")
    size_two = jnp.sqrt(norm_sq + 1e-06)
    second = remain / size_two[None, None, :, None]
    factor = 1.0 / (total_clusters * width)
    arnoldi = jnp.stack([beta * jnp.sqrt(jnp.float32(factor)), proj_re, proj_im, size_two], axis=0)
    image_two = operate(second)
    g12r, g12i = inner(image_one, image_two)
    q1r, q1i = inner(image_one, base)
    q2r, q2i = inner(image_two, base)
    g11, g22, g12r, g12i, q1r, q1i, q2r, q2i = lax.psum(
        (squares(image_one), squares(image_two), g12r, g12i, q1r, q1i, q2r, q2i), "clus"
    )
    det = g11 * g22 - (g12r * g12r + g12i * g12i)
    y1r = (g22 * q1r - (g12r * q2r - g12i * q2i)) / det
    y1i = (g22 * q1i - (g12r * q2i + g12i * q2r)) / det
    y2r = (g11 * q2r - (g12r * q1r + g12i * q1i)) / det
    y2i = (g11 * q2i - (g12r * q1i - g12i * q1r)) / det
    iterate = scaled(first, y1r, y1i) + scaled(second, y2r, y2i)
    wr = weight[0]
    wi = weight[1]
    solution = jnp.stack(
        [wr * iterate[:, 0] - wi * iterate[:, 1], wr * iterate[:, 1] + wi * iterate[:, 0]], axis=1
    )
    high = lax.Precision.HIGHEST
    mom_re = jnp.einsum("npr,nqr->pq", base[:, 0], iterate[:, 0], precision=high) + jnp.einsum(
        "npr,nqr->pq", base[:, 1], iterate[:, 1], precision=high
    )
    mom_im = jnp.einsum("npr,nqr->pq", base[:, 0], iterate[:, 1], precision=high) - jnp.einsum(
        "npr,nqr->pq", base[:, 1], iterate[:, 0], precision=high
    )
    mom_re, mom_im = lax.psum((mom_re, mom_im), "clus")
    moment = jnp.stack([wr * mom_re - wi * mom_im, wr * mom_im + wi * mom_re], axis=0) * factor
    return (solution, moment, arnoldi)


def solution(mesh):
    in_specs = (
        P("clus", None, None, None),
        P(("contour", "clus"), None, None, None, None),
        P("clus", None),
        P("clus"),
        P("clus"),
        P(("contour", "clus"), None, None, None),
        P(("contour", "clus"), None, None, None),
        P("clus", None),
        P(("contour", "clus"), None, None, None, None),
        P("contour"),
    )
    out_specs = (
        P(("contour", "clus"), None, None, None),
        P("contour", None, None),
        P("contour", None),
    )
    return jax.shard_map(shards, mesh=mesh, in_specs=in_specs, out_specs=out_specs, check_vma=False)
```

profile of v0, /device:TPU:0, one launch (start us, length us, event | category | flops | bytes accessed | tf_op | source)
XLA Modules:
  0.0 565.3 jit_solution(2159509121463575209)
XLA Ops:
  9.0 68.7 %psum.98 = f32[16]{0:T(128)S(1)} all-reduce(f32[16]{0:T(128)S(1)} %get-tuple-element.43), channel_id=1, replica_groups=mesh['contour'=4,'clus'=32] {'clus'}, use_global_device_ids=true, to_apply=%region_1.0 | all-reduce | flops 16 | bytes 128 | tf_op jit(solution)/shard_map/psum | solution.py:128
  79.1 3.0 collective-permute-start
  92.9 5.5 fusion.51
  99.0 2.0 fusion.48
  101.0 2.0 fusion.119
  103.0 2.0 fusion.125
  105.1 21.4 %all-gather.3.cloned.1.call-done = f32[256,2,512]{2,0,1:T(8,128)} async-done(((f32[8,2,512]{2,0,1:T(8,128)}), f32[256,2,512]{2,0,1:T(8,128)}) %all-gather.3.cloned.1.call-update) | async-done | bytes 1048592 | tf_op jit(solution)/shard_map/all_gather | solution.py:119
  128.0 4.4 copy.34
  132.4 5.0 gather_fusion.1
  137.4 2.6 copy.35
  142.4 3.7 fusion.83
  146.1 3.7 fusion.80
  149.8 3.7 fusion.143
  153.6 3.9 fusion.140
  158.2 65.2 %all-reduce.2 = (f32[16]{0:T(128)S(1)}, f32[16]{0:T(128)S(1)}) all-reduce(f32[16]{0:T(128)S(1)} %get-tuple-element.18, f32[16]{0:T(128)S(1)} %get-tuple-element.17), channel_id=1, replica_groups=mesh['contour'=4,'clus'=32] {'clus'}, use_global_device_ids=true, to_apply=%region_5.8 | all-reduce | flops 32 | bytes 256 | tf_op jit(solution)/shard_map/psum | solution.py:132
  223.6 62.7 %psum.101 = f32[16]{0:T(128)S(1)} all-reduce(f32[16]{0:T(128)S(1)} %get-tuple-element.22), channel_id=1, replica_groups=mesh['contour'=4,'clus'=32] {'clus'}, use_global_device_ids=true, to_apply=%region_7.10 | all-reduce | flops 16 | bytes 128 | tf_op jit(solution)/shard_map/psum | solution.py:134
  288.0 3.0 collective-permute-start.2
  295.1 5.2 fusion.57
  300.3 5.2 fusion.54
  305.5 5.2 fusion.107
  310.7 2.0 fusion.113
  312.7 19.7 %all-gather.5.cloned.1.call-done = f32[256,2,512]{2,0,1:T(8,128)} async-done(((f32[8,2,512]{2,0,1:T(8,128)}), f32[256,2,512]{2,0,1:T(8,128)}) %all-gather.5.cloned.1.call-update) | async-done | bytes 1048592 | tf_op jit(solution)/shard_map/all_gather | solution.py:119
  333.9 4.4 copy.44
  338.3 5.0 gather_fusion.3
  343.3 2.6 copy.45
  346.7 1.6 slice-done.3
  348.3 3.7 fusion.89
  352.0 3.7 fusion.86
  355.8 3.7 fusion.149
  359.6 4.0 fusion.146
  364.4 65.2 %all-reduce.1 = (f32[16]{0:T(128)S(1)}, f32[16]{0:T(128)S(1)}, f32[16]{0:T(128)S(1)}, f32[16]{0:T(128)S(1)}, f32[16]{0:T(128)S(1)}, /*index=5*/f32[16]{0:T(128)S(1)}, f32[16]{0:T(128)S(1)}, f32[16]{0:T(128)S(1)}) all-reduce(f32[16]{0:T(128)S(1)} %get-tuple-element.45, ...), channel_id=1, replica_groups=mesh['contour'=4,'clus'=32] {'clus'}, use_global_device_ids=true, to_apply=%region_17.20 | all-reduce | flops 128 | bytes 1024 | tf_op jit(solution)/shard_map/psum | solution.py:143
  432.6 123.8 %all-reduce = (f32[16,16]{1,0:T(8,128)S(1)}, f32[16,16]{1,0:T(8,128)S(1)}) all-reduce(f32[16,16]{1,0:T(8,128)S(1)} %fusion.152, f32[16,16]{1,0:T(8,128)S(1)} %fusion.153), channel_id=1, replica_groups=mesh['contour'=4,'clus'=32] {'clus'}, use_global_device_ids=true, to_apply=%region_24.27 | all-reduce | flops 512 | bytes 4096 | tf_op jit(solution)/shard_map/psum | solution.py:164
  (106 shorter events, 33.1 us)
Async XLA Ops:
  7.2 119.3 %all-gather.3.cloned.1.call-start = ((), (), s32[]{:S(2)}) async-start(), calls=%async_computation | async-start | bytes 1081344 | tf_op jit(solution)/shard_map/all_gather | solution.py:119
  77.8 13.1 %collective-permute-start.1 = (bf16[8,2,16,128]{3,2,0,1:T(8,128)(2,1)S(1)}, bf16[8,2,16,128]{3,2,0,1:T(8,128)(2,1)S(1)}, u32[]{:S(2)}, u32[]{:S(2)}) collective-permute-start(bf16[8,2,16,128]{3,2,0,1:T(8,128)(2,1)S(1)} %get-tuple-element.41), channel_id=1, source_target_pairs={{1,0},{2,1},{3,2},{4,3},{5,4},{6,5},{7,6},{8,7},{9,8},{10,9},{11,1... | collective-permute-start | bytes 196616 | tf_op jit(solution)/shard_map/ppermute | solution.py:17
  79.1 11.8 %collective-permute-start = (bf16[8,2,16,128]{3,2,0,1:T(8,128)(2,1)S(1)}, bf16[8,2,16,128]{3,2,0,1:T(8,128)(2,1)S(1)}, u32[]{:S(2)}, u32[]{:S(2)}) collective-permute-start(bf16[8,2,16,128]{3,2,0,1:T(8,128)(2,1)S(1)} %get-tuple-element.41), channel_id=1, source_target_pairs={{0,1},{1,2},{2,3},{3,4},{4,5},{5,6},{6,7},{7,8},{8,9},{9,10},{10,1... | collective-permute-start | bytes 196616 | tf_op jit(solution)/shard_map/ppermute | solution.py:15
  87.2 245.2 %all-gather.5.cloned.1.call-start = ((), (), s32[]{:S(2)}) async-start(), calls=%async_computation.1 | async-start | bytes 1081344 | tf_op jit(solution)/shard_map/all_gather | solution.py:119
  91.9 7.1 %copy-start.2 = (bf16[8,27,2,128,128]{4,3,2,1,0:T(8,128)(2,1)S(1)}, bf16[8,27,2,128,128]{4,3,2,1,0:T(8,128)(2,1)}, u32[]{:S(2)}) copy-start(bf16[8,27,2,128,128]{4,3,2,1,0:T(8,128)(2,1)} %param.15) | copy-start | bytes 42467332
  137.3 3.7 slice-start
  140.0 2.4 slice-start.1
  153.5 3.9 copy-start.1
  153.6 132.8 %copy-start = (bf16[8,2,32,128]{3,2,1,0:T(8,128)(2,1)S(1)}, bf16[8,2,32,128]{3,2,1,0:T(8,128)(2,1)}, u32[]{:S(2)}) copy-start(bf16[8,2,32,128]{3,2,1,0:T(8,128)(2,1)} %param.20) | copy-start | bytes 393220
  286.7 6.3 %collective-permute-start.3 = (bf16[8,2,16,128]{3,2,0,1:T(8,128)(2,1)S(1)}, bf16[8,2,16,128]{3,2,0,1:T(8,128)(2,1)S(1)}, u32[]{:S(2)}, u32[]{:S(2)}) collective-permute-start(bf16[8,2,16,128]{3,2,0,1:T(8,128)(2,1)S(1)} %get-tuple-element.37), channel_id=1, source_target_pairs={{1,0},{2,1},{3,2},{4,3},{5,4},{6,5},{7,6},{8,7},{9,8},{10,9},{11,1... | collective-permute-start | bytes 196616 | tf_op jit(solution)/shard_map/ppermute | solution.py:17
  288.0 5.0 collective-permute-start.2
  295.0 15.6 %slice-start.4 = ((s8[14155776]{0:T(1024)(128)(4,1)}), s8[4194304]{0:T(1024)(128)(4,1)S(1)}, s32[]{:S(2)}) async-start(s8[14155776]{0:T(1024)(128)(4,1)} %bitcast.486), calls=%async_computation.6 | async-start | bytes 8388608
  295.1 15.6 %slice-start.5 = ((s8[14155776]{0:T(1024)(128)(4,1)}), s8[4194304]{0:T(1024)(128)(4,1)S(1)}, s32[]{:S(2)}) async-start(s8[14155776]{0:T(1024)(128)(4,1)} %bitcast.486), calls=%async_computation.7 | async-start | bytes 8388608
  300.2 10.4 %slice-start.6 = ((s8[14155776]{0:T(1024)(128)(4,1)}), s8[4194304]{0:T(1024)(128)(4,1)S(1)}, s32[]{:S(2)}) async-start(s8[14155776]{0:T(1024)(128)(4,1)} %bitcast.486), calls=%async_computation.8 | async-start | bytes 8388608
  305.4 5.2 slice-start.7
  343.3 3.4 slice-start.2
  345.9 2.4 slice-start.3
Sparse Core Ops, SparseCore 0:
  87.3 39.0 all-gather.2
  292.6 39.7 all-gather.4
where the time goes:
time: 572 us; the launch traced here: 565 us
  blocking collectives  386 us (67%)
  matrix products  65.8 us (12%)
  waiting for transfers between devices  41.1 us (7%)
  local copies, waits for them, and re-layouts  36.3 us (6%)
  between operations  14.7 us (3%)
  other arithmetic  13.1 us (2%)
  starting transfers between devices  8.74 us (2%)
    psum x1, blocking collectives, shards(): mom_re, mom_im = lax.psum((mom_re, mom_im), 'clus')  124 us
    psum x1, blocking collectives, shards(): beta = jnp.sqrt(lax.psum(squares(base), 'clus') + 1e-06)  68.7 us
    psum x1, blocking collectives, shards(): lax.psum((squares(image_one), squares(image_two), g12r, g12i, q1r, q1i, q...  65.2 us
    psum x1, blocking collectives, shards(): proj_re, proj_im = lax.psum((local_re, local_im), 'clus')  65.2 us
    psum x1, blocking collectives, shards(): norm_sq = lax.psum(squares(remain), 'clus')  62.7 us
    all_gather x2, waiting for transfers between devices, operate(): whole = lax.all_gather(coef, 'clus', axis=0, tiled=True)  41 us
    dot_general x8, matrix products, couple(): return jnp.einsum('nfqs,nfsp->nqp', mat, vec, precision=high)  30.2 us
    dot_general x8, matrix products, prod(): jnp.einsum('nkrs,nkps->npr', mat, vec, preferred_element_type=jnp.float32)  29.1 us
  transfers between devices with their start and end apart: 6, of which 2 were waited for; matrix products, arithmetic and copies ran while one was open for 8% of the time, Pallas kernels for 0%

commit v1 on v0

--- a/solution.py
+++ b/solution.py
@@ -116,7 +116,9 @@
         pulled = jnp.where(slot_live[:, :, None, None, None], pulled, jnp.zeros((), jnp.bfloat16))
         near = block_product(near_blocks, pulled)
         coef = basis_contract(col_basis, narrow)
-        whole = lax.all_gather(coef, "clus", axis=0, tiled=True)
+        whole = jnp.concatenate(
+            lax.all_to_all(jnp.stack([coef] * lax.axis_size("clus")), "clus", 0, 0), axis=0
+        )
         whole = whole.reshape(whole.shape[0], 2, rank, nprobe)
         taken = jnp.take(whole, far_list, axis=0)
         farcoef = far_couple(far_coupling, taken)

time: 572 us -> 543 us (0.949)
  waiting for transfers between devices: 41.1 us -> 1.72 us
  local copies, waits for them, and re-layouts: 36.3 us -> 49.6 us
  between operations: 14.7 us -> 1.5 us
  starting transfers between devices: 8.74 us -> 16.5 us
    all_gather x2 -> x0, waiting for transfers between devices: 41 us -> none  [operate(): whole = lax.all_gather(coef, 'clus', axis=0, tiled=True)]
    another operation x0 -> x6, local copies, waits for them, and re-layouts: none -> 25.6 us  [the longest x4 23.4 us: operate(): whole = whole.reshape(whole.shape[0], 2, rank, nprobe)]
    reshape x2 -> x0, local copies, waits for them, and re-layouts: 8.75 us -> none  [operate(): whole = whole.reshape(whole.shape[0], 2, rank, nprobe)]
    all_to_all x0 -> x2, starting transfers between devices: none -> 7.86 us  [operate(): lax.all_to_all(jnp.stack([coef] * lax.axis_size('clus')), 'clus', 0, 0)]
  transfers between devices with their start and end apart: 6 -> 6, of which waited for: 2 -> 1; matrix products, arithmetic and copies ran while one was open for 8% -> 8% of each run, Pallas kernels for 0% -> 0%
where the time goes in v1:
time: 543 us; the launch traced here: 536 us
  blocking collectives  389 us (72%)
  matrix products  65.6 us (12%)
  local copies, waits for them, and re-layouts  49.6 us (9%)
  starting transfers between devices  16.5 us (3%)
  other arithmetic  12.4 us (2%)
    psum x1, blocking collectives, shards(): mom_re, mom_im = lax.psum((mom_re, mom_im), 'clus')  124 us
    psum x1, blocking collectives, shards(): beta = jnp.sqrt(lax.psum(squares(base), 'clus') + 1e-06)  68.7 us
    psum x1, blocking collectives, shards(): lax.psum((squares(image_one), squares(image_two), g12r, g12i, q1r, q1i, q...  67.6 us
    psum x1, blocking collectives, shards(): proj_re, proj_im = lax.psum((local_re, local_im), 'clus')  65.9 us
    psum x1, blocking collectives, shards(): norm_sq = lax.psum(squares(remain), 'clus')  62.7 us
    dot_general x8, matrix products, couple(): return jnp.einsum('nfqs,nfsp->nqp', mat, vec, precision=high)  30.2 us
    dot_general x8, matrix products, prod(): jnp.einsum('nkrs,nkps->npr', mat, vec, preferred_element_type=jnp.float32)  29 us
    another operation x4, local copies, waits for them, and re-layouts, operate(): whole = whole.reshape(whole.shape[0], 2, rank, nprobe)  23.4 us
  transfers between devices with their start and end apart: 6, of which 1 were waited for; matrix products, arithmetic and copies ran while one was open for 8% of the time, Pallas kernels for 0%

profile of v1, /device:TPU:0, one launch (start us, length us, event | category | flops | bytes accessed | tf_op | source)
XLA Modules:
  0.0 536.0 jit_solution(11849020375329644086)
XLA Ops:
  2.5 68.7 %psum.98 = f32[16]{0:T(128)S(1)} all-reduce(f32[16]{0:T(128)S(1)} %get-tuple-element.46), channel_id=1, replica_groups=mesh['contour'=4,'clus'=32] {'clus'}, use_global_device_ids=true, to_apply=%region_1.0 | all-reduce | flops 16 | bytes 128 | tf_op jit(solution)/shard_map/psum | solution.py:130
  73.1 3.0 collective-permute-start
  81.7 3.9 all-to-all-start
  88.6 5.4 %fusion.51 = f32[8,16,128]{2,1,0:T(8,128)S(1)} fusion(bf16[8,27,2,128,128]{4,3,2,1,0:T(8,128)(2,1)} %param.15, bf16[8,27,2,16,128]{4,3,1,0,2:T(8,128)(2,1)S(1)} %select_select_fusion.1), kind=kOutput, calls=%fused_computation.61 | convolution fusion | flops 113246208 | bytes 8028160 | tf_op jit(solution)/shard_map/nkrs,nkps->npr/dot_general | solution.py:27
  94.6 2.0 fusion.119
  96.6 2.0 fusion.48
  98.6 2.0 fusion.125
  102.4 4.9 reshape_reshape.6
  107.3 6.8 %copy.54 = f32[256,2,32,16]{2,3,1,0:T(8,128)} copy(f32[256,2,32,16]{3,2,0,1:T(8,128)} %reshape_reshape.6) | data formatting | bytes 2097152 | tf_op jit(solution)/shard_map/reshape;reshape | solution.py:122
  114.2 4.9 gather_fusion.1
  119.1 2.6 copy.55
  124.1 3.7 fusion.83
  127.8 3.7 fusion.80
  131.6 3.7 fusion.143
  135.3 3.9 fusion.140
  140.0 65.9 %all-reduce.2 = (f32[16]{0:T(128)S(1)}, f32[16]{0:T(128)S(1)}) all-reduce(f32[16]{0:T(128)S(1)} %get-tuple-element.21, f32[16]{0:T(128)S(1)} %get-tuple-element.20), channel_id=1, replica_groups=mesh['contour'=4,'clus'=32] {'clus'}, use_global_device_ids=true, to_apply=%region_5.8 | all-reduce | flops 32 | bytes 256 | tf_op jit(solution)/shard_map/psum | solution.py:134
  206.6 62.7 %psum.101 = f32[16]{0:T(128)S(1)} all-reduce(f32[16]{0:T(128)S(1)} %get-tuple-element.25), channel_id=1, replica_groups=mesh['contour'=4,'clus'=32] {'clus'}, use_global_device_ids=true, to_apply=%region_7.10 | all-reduce | flops 16 | bytes 128 | tf_op jit(solution)/shard_map/psum | solution.py:136
  271.6 3.0 collective-permute-start.2
  276.5 3.9 all-to-all-start.1
  283.8 5.2 fusion.57
  289.0 5.2 fusion.107
  294.2 5.2 fusion.54
  301.5 4.9 reshape_reshape.7
  306.4 6.8 %copy.64 = f32[256,2,32,16]{2,3,1,0:T(8,128)} copy(f32[256,2,32,16]{3,2,0,1:T(8,128)} %reshape_reshape.7) | data formatting | bytes 2097152 | tf_op jit(solution)/shard_map/reshape;reshape | solution.py:122
  313.2 4.9 gather_fusion.3
  318.1 2.6 copy.65
  323.2 3.7 fusion.89
  326.9 3.7 fusion.86
  330.6 3.7 fusion.149
  334.5 4.0 fusion.146
  339.3 67.6 %all-reduce.1 = (f32[16]{0:T(128)S(1)}, f32[16]{0:T(128)S(1)}, f32[16]{0:T(128)S(1)}, f32[16]{0:T(128)S(1)}, f32[16]{0:T(128)S(1)}, /*index=5*/f32[16]{0:T(128)S(1)}, f32[16]{0:T(128)S(1)}, f32[16]{0:T(128)S(1)}) all-reduce(f32[16]{0:T(128)S(1)} %get-tuple-element.48, ...), channel_id=1, replica_groups=mesh['contour'=4,'clus'=32] {'clus'}, use_global_device_ids=true, to_apply=%region_17.20 | all-reduce | flops 128 | bytes 1024 | tf_op jit(solution)/shard_map/psum | solution.py:145
  410.0 123.8 %all-reduce = (f32[16,16]{1,0:T(8,128)S(1)}, f32[16,16]{1,0:T(8,128)S(1)}) all-reduce(f32[16,16]{1,0:T(8,128)S(1)} %fusion.152, f32[16,16]{1,0:T(8,128)S(1)} %fusion.153), channel_id=1, replica_groups=mesh['contour'=4,'clus'=32] {'clus'}, use_global_device_ids=true, to_apply=%region_24.27 | all-reduce | flops 512 | bytes 4096 | tf_op jit(solution)/shard_map/psum | solution.py:166
  (126 shorter events, 36.1 us)
Async XLA Ops:
  0.6 85.0 %copy-start.3 = (s32[8,32]{1,0:T(8,128)S(1)}, s32[8,32]{1,0:T(8,128)}, u32[]{:S(2)}) copy-start(s32[8,32]{1,0:T(8,128)} %param.21) | copy-start | bytes 3076
  0.6 85.0 %copy-start.6 = (s32[8,27]{1,0:T(8,128)S(1)}, s32[8,27]{1,0:T(8,128)}, u32[]{:S(2)}) copy-start(s32[8,27]{1,0:T(8,128)} %param.16) | copy-start | bytes 2596
  0.7 85.0 %copy-start.9 = (s32[8]{0:T(128)S(1)}, s32[8]{0:T(128)}, u32[]{:S(2)}) copy-start(s32[8]{0:T(128)} %param.17) | copy-start | bytes 100
  0.7 85.2 %copy-start.8 = (f32[2]{0:T(128)S(1)}, f32[2]{0:T(128)}, u32[]{:S(2)}) copy-start(f32[2]{0:T(128)} %param.23) | copy-start | bytes 28
  71.8 14.8 %collective-permute-start.1 = (bf16[8,2,16,128]{3,2,0,1:T(8,128)(2,1)S(1)}, bf16[8,2,16,128]{3,2,0,1:T(8,128)(2,1)S(1)}, u32[]{:S(2)}, u32[]{:S(2)}) collective-permute-start(bf16[8,2,16,128]{3,2,0,1:T(8,128)(2,1)S(1)} %get-tuple-element.44), channel_id=1, source_target_pairs={{1,0},{2,1},{3,2},{4,3},{5,4},{6,5},{7,6},{8,7},{9,8},{10,9},{11,1... | collective-permute-start | bytes 196616 | tf_op jit(solution)/shard_map/ppermute | solution.py:17
  73.1 13.5 %collective-permute-start = (bf16[8,2,16,128]{3,2,0,1:T(8,128)(2,1)S(1)}, bf16[8,2,16,128]{3,2,0,1:T(8,128)(2,1)S(1)}, u32[]{:S(2)}, u32[]{:S(2)}) collective-permute-start(bf16[8,2,16,128]{3,2,0,1:T(8,128)(2,1)S(1)} %get-tuple-element.44), channel_id=1, source_target_pairs={{0,1},{1,2},{2,3},{3,4},{4,5},{5,6},{6,7},{7,8},{8,9},{9,10},{10,1... | collective-permute-start | bytes 196616 | tf_op jit(solution)/shard_map/ppermute | solution.py:15
  81.7 20.7 %all-to-all-start = ((f32[32,8,2,512]{3,1,2,0:T(8,128)}), f32[32,8,2,512]{3,1,2,0:T(8,128)S(1)}, u32[]{:S(2)}, u32[]{:S(2)}) async-start(f32[32,8,2,512]{3,1,2,0:T(8,128)} %stack.66), calls=%async_computation | async-start | bytes 2097152 | tf_op jit(solution)/shard_map/all_to_all | solution.py:120
  85.7 2.8 copy-start.4
  85.7 2.8 copy-start.5
  87.6 7.1 %copy-start.11 = (bf16[8,27,2,128,128]{4,3,2,1,0:T(8,128)(2,1)S(1)}, bf16[8,27,2,128,128]{4,3,2,1,0:T(8,128)(2,1)}, u32[]{:S(2)}) copy-start(bf16[8,27,2,128,128]{4,3,2,1,0:T(8,128)(2,1)} %param.15) | copy-start | bytes 42467332
  119.1 3.7 slice-start
  121.7 2.4 slice-start.1
  135.3 3.9 copy-start.1
  135.3 134.7 %copy-start = (bf16[8,2,32,128]{3,2,1,0:T(8,128)(2,1)S(1)}, bf16[8,2,32,128]{3,2,1,0:T(8,128)(2,1)}, u32[]{:S(2)}) copy-start(bf16[8,2,32,128]{3,2,1,0:T(8,128)(2,1)} %param.20) | copy-start | bytes 393220
  139.2 141.2 %copy-start.10 = (f32[1,16]{1,0:T(1,128)S(1)}, f32[1,16]{1,0:T(1,128)}, u32[]{:S(2)}) copy-start(f32[1,16]{1,0:T(1,128)} %get-tuple-element.64) | copy-start | bytes 196
  270.3 10.8 %collective-permute-start.3 = (bf16[8,2,16,128]{3,2,0,1:T(8,128)(2,1)S(1)}, bf16[8,2,16,128]{3,2,0,1:T(8,128)(2,1)S(1)}, u32[]{:S(2)}, u32[]{:S(2)}) collective-permute-start(bf16[8,2,16,128]{3,2,0,1:T(8,128)(2,1)S(1)} %get-tuple-element.40), channel_id=1, source_target_pairs={{1,0},{2,1},{3,2},{4,3},{5,4},{6,5},{7,6},{8,7},{9,8},{10,9},{11,1... | collective-permute-start | bytes 196616 | tf_op jit(solution)/shard_map/ppermute | solution.py:17
  271.6 9.4 %collective-permute-start.2 = (bf16[8,2,16,128]{3,2,0,1:T(8,128)(2,1)S(1)}, bf16[8,2,16,128]{3,2,0,1:T(8,128)(2,1)S(1)}, u32[]{:S(2)}, u32[]{:S(2)}) collective-permute-start(bf16[8,2,16,128]{3,2,0,1:T(8,128)(2,1)S(1)} %get-tuple-element.40), channel_id=1, source_target_pairs={{0,1},{1,2},{2,3},{3,4},{4,5},{5,6},{6,7},{7,8},{8,9},{9,10},{10,1... | collective-permute-start | bytes 196616 | tf_op jit(solution)/shard_map/ppermute | solution.py:15
  276.5 24.9 %all-to-all-start.1 = ((f32[32,8,2,512]{3,1,2,0:T(8,128)}), f32[32,8,2,512]{3,1,2,0:T(8,128)S(1)}, u32[]{:S(2)}, u32[]{:S(2)}) async-start(f32[32,8,2,512]{3,1,2,0:T(8,128)} %stack.75), calls=%async_computation.1 | async-start | bytes 2097152 | tf_op jit(solution)/shard_map/all_to_all | solution.py:120
  283.8 15.6 %slice-start.4 = ((s8[14155776]{0:T(1024)(128)(4,1)}), s8[4194304]{0:T(1024)(128)(4,1)S(1)}, s32[]{:S(2)}) async-start(s8[14155776]{0:T(1024)(128)(4,1)} %bitcast.490), calls=%async_computation.6 | async-start | bytes 8388608
  283.8 15.6 %slice-start.5 = ((s8[14155776]{0:T(1024)(128)(4,1)}), s8[4194304]{0:T(1024)(128)(4,1)S(1)}, s32[]{:S(2)}) async-start(s8[14155776]{0:T(1024)(128)(4,1)} %bitcast.490), calls=%async_computation.7 | async-start | bytes 8388608
  289.0 10.4 %slice-start.6 = ((s8[14155776]{0:T(1024)(128)(4,1)}), s8[4194304]{0:T(1024)(128)(4,1)S(1)}, s32[]{:S(2)}) async-start(s8[14155776]{0:T(1024)(128)(4,1)} %bitcast.490), calls=%async_computation.8 | async-start | bytes 8388608
  294.2 5.2 slice-start.7
  318.1 3.4 slice-start.2
  320.8 2.4 slice-start.3
  334.3 4.9 copy-start.7
  334.3 72.6 %copy-start.2 = (f32[8,2,16,128]{3,2,0,1:T(8,128)S(1)}, f32[8,2,16,128]{3,2,0,1:T(8,128)}, u32[]{:S(2)}) copy-start(f32[8,2,16,128]{3,2,0,1:T(8,128)} %get-tuple-element.41) | copy-start | bytes 393220
